TPU v7x, 512 devices: a whole 4x8x8 slice. The times are simulated.
512 devices in a mesh: rep: 32 (over x, y), tp: 16 (over z, core).
Axes of the slice: x: 4, y: 8, z: 8, core: 2. Of those that a mesh axis runs over, the one named last changes fastest.
Arguments:
- queries: bfloat16 [416, 48, 4096], P('rep', None, 'tp'), may hold values from -33 to 33
- tree_cache: bfloat16 [416, 2, 48, 4096], P('rep', None, None, 'tp'), may hold values from -11 to 11
- tree_mask: int32 [416, 48, 48], P('rep'), may hold values from 0 to 1, as said below
- dest_group: int32 [416, 1], P('rep'), may hold values from 0 to 31; in each aligned block of 13 rows (0 to 12, 13 to 25, ...) at most 2 rows name the same one
- accepted_path: int32 [416, 8], P('rep'), may hold values from 0 to 47
- prompt_cache: bfloat16 [32, 2, 152, 4096], P('rep', None, None, 'tp'), may hold values from -11 to 11
- first_len: int32 [32], P('rep'), may hold values from 2 to 152
- spill_cache: bfloat16 [32, 2, 152, 4096], P('rep', None, None, 'tp'), may hold values from -6 to 6
- spill_len: int32 [32], P('rep'), may hold values from 76 to 152
- out_weight: bfloat16 [4096, 4096], P(None, 'tp'), may hold values from -0.09375 to 0.09375
Outputs:
- projected: bfloat16 [416, 48, 4096], P('rep', None, 'tp')
- accepted_cache: bfloat16 [416, 2, 8, 4096], P('rep', None, None, 'tp')
Inputs may be any that keep to these rules, and one draw needn't show every extreme that they name: `dest_group`: in each aligned block of 13 requests (those of one index of rep) no group is named more than 2 times. Row t of tree_mask[r] marks token t and its ancestors in a tree whose parents come before their children.
All inputs are finite; a program needn't handle non-finite values.
Results may differ from a plain program's by a relative error of at most 0.014.
Values may be sent and summed in bfloat16 or wider, within the bound.
A program may use at most 64 MiB of HBM per device.

v0:
```python
import math
import jax
import jax.numpy as jnp
from jax import lax
from jax.sharding import PartitionSpec as P

HD = 128
TREE = 48
PCAP = 152
NEG_FILL = -1e30


def swapped(value, axis, apart):
    mask = 2**apart
    pairs = [(source, source ^ mask) for source in range(lax.axis_size(axis))]
    return lax.ppermute(value, axis, pairs)


def split_heads(rows):
    return rows.reshape(rows.shape[:-1] + (rows.shape[-1] // HD, HD))


def prompt_attend(query_rows, key_rows, value_rows, seen):
    q = split_heads(query_rows)
    k = split_heads(key_rows)
    v = split_heads(value_rows)
    scores = jnp.einsum("qhd,khd->hqk", q, k, preferred_element_type=jnp.float32) * (
        1.0 / math.sqrt(HD)
    )
    scores = jnp.where(seen[None, None, :], scores, NEG_FILL)
    peaks = jnp.max(scores, axis=2, keepdims=True)
    raw = jnp.where(seen[None, None, :], jnp.exp(scores - peaks), 0.0)
    totals = jnp.sum(raw, axis=2)
    accum = jnp.einsum(
        "hqk,khd->qhd", raw.astype(jnp.bfloat16), v, preferred_element_type=jnp.float32
    )
    normed = accum / jnp.transpose(totals)[:, :, None]
    lse = jnp.transpose(peaks[:, :, 0] + jnp.log(totals))
    return (normed.reshape(query_rows.shape).astype(jnp.bfloat16), lse)


def tree_attend(queries, keys, values, seen):
    q = split_heads(queries)
    k = split_heads(keys)
    v = split_heads(values)
    scores = jnp.einsum("rthd,rshd->rhts", q, k, preferred_element_type=jnp.float32) * (
        1.0 / math.sqrt(HD)
    )
    scores = jnp.where(seen[:, None], scores, NEG_FILL)
    peaks = jnp.max(scores, axis=3, keepdims=True)
    raw = jnp.where(seen[:, None], jnp.exp(scores - peaks), 0.0)
    totals = jnp.sum(raw, axis=3)
    accum = jnp.einsum(
        "rhts,rshd->rthd", raw.astype(jnp.bfloat16), v, preferred_element_type=jnp.float32
    )
    return (jnp.swapaxes(peaks[..., 0], 1, 2), jnp.swapaxes(totals, 1, 2), accum)


def local(
    queries,
    tree_cache,
    tree_mask,
    dest_group,
    accepted_path,
    prompt_cache,
    first_len,
    spill_cache,
    spill_len,
    out_weight,
):
    req_here = queries.shape[0]
    local_cols = queries.shape[2]
    heads_here = local_cols // HD
    groups = lax.axis_size("rep")
    per_group = max(2, (req_here + groups - 1) // groups)
    n_slots = groups * per_group
    positions = jnp.arange(PCAP, dtype=jnp.int32)
    live_flag = (positions < spill_len[0]).astype(jnp.bfloat16)
    partner_cache, partner_flag = swapped((spill_cache, live_flag), "rep", 0)
    target = dest_group[:, 0]
    same_target = target[:, None] == target[None, :]
    earlier = jnp.arange(req_here)[None, :] < jnp.arange(req_here)[:, None]
    rank_index = jnp.sum(jnp.logical_and(same_target, earlier), axis=1)
    slot_index = target * per_group + rank_index
    selector = (jnp.arange(n_slots, dtype=jnp.int32)[:, None] == slot_index[None, :]).astype(
        jnp.bfloat16
    )
    outbound = jnp.einsum(
        "sr,rtc->stc", selector, queries, preferred_element_type=jnp.float32
    ).astype(jnp.bfloat16)
    outbound = outbound.reshape(groups, per_group, TREE, local_cols)
    inbound = lax.all_to_all(outbound, "rep", split_axis=0, concat_axis=0, tiled=True)
    routed_rows = inbound.reshape(n_slots * TREE, local_cols)
    key_rows = jnp.concatenate([prompt_cache[0, 0], partner_cache[0, 0]], axis=0)
    value_rows = jnp.concatenate([prompt_cache[0, 1], partner_cache[0, 1]], axis=0)
    seen = jnp.concatenate([positions < first_len[0], partner_flag > 0.5], axis=0)
    normed, lse = prompt_attend(routed_rows, key_rows, value_rows, seen)
    back_out = lax.all_to_all(
        normed.reshape(groups, per_group, TREE, local_cols),
        "rep",
        split_axis=0,
        concat_axis=0,
        tiled=True,
    ).reshape(n_slots, TREE, local_cols)
    back_lse = lax.all_to_all(
        lse.reshape(groups, per_group, TREE, heads_here),
        "rep",
        split_axis=0,
        concat_axis=0,
        tiled=True,
    ).reshape(n_slots, TREE, heads_here)
    remote_out = split_heads(jnp.take(back_out, slot_index, axis=0)).astype(jnp.float32)
    remote_lse = jnp.take(back_lse, slot_index, axis=0)
    tree_max, tree_total, tree_accum = tree_attend(
        queries, tree_cache[:, 0], tree_cache[:, 1], tree_mask == 1
    )
    peaks = jnp.maximum(remote_lse, tree_max)
    factor_remote = jnp.exp(remote_lse - peaks)
    factor_tree = jnp.exp(tree_max - peaks)
    totals = factor_remote + tree_total * factor_tree
    accum = remote_out * factor_remote[..., None] + tree_accum * factor_tree[..., None]
    attn = (accum / totals[..., None]).reshape(req_here * TREE, local_cols).astype(jnp.bfloat16)
    summed = jnp.dot(
        lax.all_gather(attn, "tp", axis=1, tiled=True),
        out_weight,
        preferred_element_type=jnp.float32,
    )
    projected = summed.astype(jnp.bfloat16).reshape(req_here, TREE, out_weight.shape[1])
    accepted_cache = jnp.take_along_axis(tree_cache, accepted_path[:, None, :, None], axis=2)
    return (projected, accepted_cache)


def solution(mesh):
    return jax.shard_map(
        local,
        mesh=mesh,
        in_specs=(
            P("rep", None, "tp"),
            P("rep", None, None, "tp"),
            P("rep", None, None),
            P("rep", None),
            P("rep", None),
            P("rep", None, None, "tp"),
            P("rep"),
            P("rep", None, None, "tp"),
            P("rep"),
            P(None, "tp"),
        ),
        out_specs=(P("rep", None, "tp"), P("rep", None, None, "tp")),
        check_vma=False,
    )
```

profile of v0, /device:TPU:1, one launch (start us, length us, event | category | flops | bytes accessed | tf_op | source)
XLA Modules:
  0.0 220.9 jit_solution(4979695363435607490)
XLA Ops:
  7.2 0.0 copy-start
  7.2 0.0 copy-start.7
  7.2 0.0 copy-start.4
  7.2 1.0 convert_reduce_fusion
  8.2 0.7 multiply_add_fusion
  8.9 1.7 convolution_convert_fusion
  10.5 2.0 copy.57
  12.6 10.6 %all-to-all-start = ((bf16[32,2,48,256]{3,2,1,0:T(8,128)(2,1)}), bf16[32,2,48,256]{3,2,1,0:T(8,128)(2,1)}, u32[]{:S(2)}, u32[]{:S(2)}) async-start(bf16[32,2,48,256]{3,2,1,0:T(8,128)(2,1)} %bitcast.101), calls=%async_computation | async-start | bytes 3145728 | tf_op jit(solution)/shard_map/all_to_all | solution.py:92
  23.8 3.1 %collective-permute-start.1 = (bf16[152]{0:T(256)(128)(2,1)S(1)}, bf16[152]{0:T(256)(128)(2,1)S(1)}, u32[]{:S(2)}, u32[]{:S(2)}) collective-permute-start(bf16[152]{0:T(256)(128)(2,1)S(1)} %compare_convert_fusion), channel_id=1, source_target_pairs={{0,16},{16,0},{32,48},{48,32},{64,80},{80,64},{96,112},{112,96},{1... | collective-permute-start | bytes 920 | tf_op jit(solution)/shard_map/ppermute | solution.py:16
  26.9 0.0 copy-done.7
  26.9 2.2 %collective-permute-start = (bf16[1,2,152,256]{3,2,1,0:T(8,128)(2,1)S(1)}, bf16[1,2,152,256]{3,2,1,0:T(8,128)(2,1)S(1)}, u32[]{:S(2)}, u32[]{:S(2)}) collective-permute-start(bf16[1,2,152,256]{3,2,1,0:T(8,128)(2,1)S(1)} %copy-done.7), channel_id=1, source_target_pairs={{0,16},{16,0},{32,48},{48,32},{64,80},{80,64},{96,112},{112,96},{1... | collective-permute-start | bytes 466952 | tf_op jit(solution)/shard_map/ppermute | solution.py:16
  29.8 0.0 copy-done.4
  29.9 26.4 %collective-permute-done.1 = bf16[152]{0:T(256)(128)(2,1)S(1)} collective-permute-done((bf16[152]{0:T(256)(128)(2,1)S(1)}, bf16[152]{0:T(256)(128)(2,1)S(1)}, u32[]{:S(2)}, u32[]{:S(2)}) %collective-permute-start.1) | collective-permute-done | bytes 336 | tf_op jit(solution)/shard_map/ppermute | solution.py:16
  56.3 0.1 pad_add_fusion
  56.4 5.2 %collective-permute-done = bf16[1,2,152,256]{3,2,1,0:T(8,128)(2,1)S(1)} collective-permute-done((bf16[1,2,152,256]{3,2,1,0:T(8,128)(2,1)S(1)}, bf16[1,2,152,256]{3,2,1,0:T(8,128)(2,1)S(1)}, u32[]{:S(2)}, u32[]{:S(2)}) %collective-permute-start) | collective-permute-done | bytes 155680 | tf_op jit(solution)/shard_map/ppermute | solution.py:16
  61.7 0.0 all-to-all-done
  61.7 3.5 %reshape_reshape.3 = bf16[3072,2,128]{2,1,0:T(2,128)(2,1)} reshape(bf16[32,2,48,256]{3,2,1,0:T(8,128)(2,1)} %all-to-all-done) | data formatting | bytes 3145728 | tf_op jit(solution)/shard_map/reshape;reshape | solution.py:20
  65.3 2.7 %fusion = (f32[2,3072]{1,0:T(2,128)S(1)}, f32[2,3072,304]{1,2,0:T(8,128)S(1)}) fusion(pred[304]{0:T(512)(128)(4,1)S(1)} %pad_add_fusion, bf16[152,2,128]{2,0,1:T(8,128)(2,1)S(1)} %copy.42, bf16[152,2,128]{2,0,1:T(8,128)(2,1)S(1)} %copy.41, bf16[3072,2,128]{2,1,0:T(2,128)(2,1)} %reshape_reshape.3), kind=kOutput, calls=%fused_computation.5 | convolution fusion | flops 484059136 | bytes 9224496 | tf_op jit(solution)/shard_map/qhd,khd->hqk/dot_general | solution.py:27
  67.9 0.0 copy-start.1
  67.9 3.0 %copy-done.1 = f32[2,3072,304]{1,2,0:T(8,128)} copy-done((f32[2,3072,304]{1,2,0:T(8,128)}, f32[2,3072,304]{1,2,0:T(8,128)S(1)}, u32[]{:S(2)}) %copy-start.1) | copy-done | bytes 7471128
  70.9 2.0 fusion.1
  72.9 0.2 reshape.85
  73.1 0.1 copy.83
  73.2 0.8 reshape.118
  73.9 9.1 %all-to-all-start.2 = ((f32[32,1,192]{2,1,0:T(1,128)}), f32[32,1,192]{2,1,0:T(1,128)S(1)}, u32[]{:S(2)}, u32[]{:S(2)}) async-start(f32[32,1,192]{2,1,0:T(1,128)} %reshape.118), calls=%async_computation.2 | async-start | bytes 65536 | tf_op jit(solution)/shard_map/all_to_all | solution.py:105
  83.0 6.4 %divide_convert_fusion = bf16[3072,2,128]{0,2,1:T(8,128)(2,1)} fusion(f32[2,3072,304]{1,2,0:T(8,128)} %copy-done.1, f32[2,3072]{1,0:T(2,128)S(1)} %get-tuple-element.17, pred[304]{0:T(512)(128)(4,1)S(1)} %pad_add_fusion, f32[3072,2]{0,1:T(2,128)S(1)} %bitcast.106, bf16[152,2,128]{2,0,1:T(8,128)(2,1)S(1)} %copy.38, bf16[152,2,128]{2,0,1:T(8,128)(2,1)S(1)} %copy.37), kind=kOutput, calls=%fused_computation.14 | convolution fusion | flops 489373696 | bytes 9249072 | tf_op jit(solution)/shard_map/hqk,khd->qhd/dot_general | solution.py:34
  89.4 5.0 %copy.44 = bf16[3072,2,128]{2,1,0:T(2,128)(2,1)} copy(bf16[3072,2,128]{0,2,1:T(8,128)(2,1)} %divide_convert_fusion) | data formatting | bytes 3145728 | tf_op jit(solution)/shard_map/convert_element_type | solution.py:39
  94.4 3.8 %convert_element_type.40 = bf16[32,2,48,256]{3,2,1,0:T(8,128)(2,1)} reshape(bf16[3072,2,128]{2,1,0:T(2,128)(2,1)} %copy.44) | data formatting | bytes 3145728 | tf_op jit(solution)/shard_map/convert_element_type | solution.py:39
  98.2 0.0 all-to-all-done.2
  98.2 9.3 %all-to-all-start.1 = ((bf16[32,2,48,256]{3,2,1,0:T(8,128)(2,1)}), bf16[32,2,48,256]{3,2,1,0:T(8,128)(2,1)}, u32[]{:S(2)}, u32[]{:S(2)}) async-start(bf16[32,2,48,256]{3,2,1,0:T(8,128)(2,1)} %convert_element_type.40), calls=%async_computation.1 | async-start | bytes 3145728 | tf_op jit(solution)/shard_map/all_to_all | solution.py:98
  107.5 0.0 copy-done.5
  107.6 0.2 all-gather.2.cloned.1.call-start
  107.8 0.0 copy-done.3
  107.8 0.2 copy.47
  108.1 0.0 copy-done.2
  108.1 0.8 reshape_squeeze.6
  108.9 0.8 reshape_squeeze.7
  109.7 0.0 copy-done.6
  109.7 0.6 and_bitcast_fusion
  110.3 0.6 pad_clamp_fusion
  110.9 1.4 fusion.54
  112.3 0.8 fusion.18
  113.1 0.5 broadcast.91
  113.6 2.0 reduce
  115.6 0.9 reshape.119
  116.5 0.7 gather_fusion.1
  117.2 0.8 fusion.38
  118.0 26.3 %all-to-all-done.1 = bf16[32,2,48,256]{3,2,1,0:T(8,128)(2,1)} async-done(((bf16[32,2,48,256]{3,2,1,0:T(8,128)(2,1)}), bf16[32,2,48,256]{3,2,1,0:T(8,128)(2,1)}, u32[]{:S(2)}, u32[]{:S(2)}) %all-to-all-start.1) | async-done | bytes 1572896 | tf_op jit(solution)/shard_map/all_to_all | solution.py:98
  144.4 2.8 %gather_fusion = bf16[13,48,256]{2,1,0:T(8,128)(2,1)} fusion(bf16[64,48,256]{2,1,0:T(8,128)(2,1)} %bitcast.9, s32[1024]{0:T(1024)} %pad_clamp_fusion), kind=kCustom, calls=%fused_computation | custom fusion | bytes 639028 | tf_op jit(solution)/shard_map/jit(_take)/gather | solution.py:112
  147.2 1.8 fusion.17
  149.0 0.2 copy.52
  149.2 0.8 copy.82
  150.0 0.0 all-gather.2.cloned.1.call-update
  150.0 0.7 bitcast_or_fusion
  150.7 0.1 copy.54
  150.8 0.1 reshape.106
  150.9 1.6 gather_fusion.2
  152.5 0.7 compare_and_fusion
  153.2 0.1 copy.53
  153.3 0.1 fusion.35
  153.4 0.7 copy.55
  154.1 55.3 %all-gather.2.cloned.1.call-done = bf16[624,4096]{1,0:T(8,128)(2,1)} async-done(((bf16[624,256]{1,0:T(8,128)(2,1)}), bf16[624,4096]{1,0:T(8,128)(2,1)}) %all-gather.2.cloned.1.call-update) | async-done | bytes 5111824 | tf_op jit(solution)/shard_map/all_gather | solution.py:124
  209.4 0.0 copy-done
  209.4 4.7 %convolution_convert_fusion.1 = bf16[624,256]{1,0:T(8,128)(2,1)} fusion(bf16[624,4096]{1,0:T(8,128)(2,1)} %all-gather.2.cloned.1.call-done, bf16[4096,256]{1,0:T(8,128)(2,1)S(1)} %copy-done), kind=kOutput, calls=%fused_computation.25 | convolution fusion | flops 1308782592 | bytes 7528448 | tf_op jit(solution)/shard_map/dot_general | solution.py:123
  (20 shorter events, 0.3 us)
Async XLA Ops:
  7.2 202.3 %copy-start = (bf16[4096,256]{1,0:T(8,128)(2,1)S(1)}, bf16[4096,256]{1,0:T(8,128)(2,1)}, u32[]{:S(2)}) copy-start(bf16[4096,256]{1,0:T(8,128)(2,1)} %param.19) | copy-start | bytes 6291460
  7.2 19.8 %copy-start.7 = (bf16[1,2,152,256]{3,2,1,0:T(8,128)(2,1)S(1)}, bf16[1,2,152,256]{3,2,1,0:T(8,128)(2,1)}, u32[]{:S(2)}) copy-start(bf16[1,2,152,256]{3,2,1,0:T(8,128)(2,1)} %param.17) | copy-start | bytes 466948
  7.2 22.6 %copy-start.4 = (bf16[1,2,152,256]{3,2,1,0:T(8,128)(2,1)S(1)}, bf16[1,2,152,256]{3,2,1,0:T(8,128)(2,1)}, u32[]{:S(2)}) copy-start(bf16[1,2,152,256]{3,2,1,0:T(8,128)(2,1)} %param.15) | copy-start | bytes 466948
  12.6 49.2 %all-to-all-start = ((bf16[32,2,48,256]{3,2,1,0:T(8,128)(2,1)}), bf16[32,2,48,256]{3,2,1,0:T(8,128)(2,1)}, u32[]{:S(2)}, u32[]{:S(2)}) async-start(bf16[32,2,48,256]{3,2,1,0:T(8,128)(2,1)} %bitcast.101), calls=%async_computation | async-start | bytes 3145728 | tf_op jit(solution)/shard_map/all_to_all | solution.py:92
  23.8 32.5 %collective-permute-start.1 = (bf16[152]{0:T(256)(128)(2,1)S(1)}, bf16[152]{0:T(256)(128)(2,1)S(1)}, u32[]{:S(2)}, u32[]{:S(2)}) collective-permute-start(bf16[152]{0:T(256)(128)(2,1)S(1)} %compare_convert_fusion), channel_id=1, source_target_pairs={{0,16},{16,0},{32,48},{48,32},{64,80},{80,64},{96,112},{112,96},{1... | collective-permute-start | bytes 920 | tf_op jit(solution)/shard_map/ppermute | solution.py:16
  26.9 34.7 %collective-permute-start = (bf16[1,2,152,256]{3,2,1,0:T(8,128)(2,1)S(1)}, bf16[1,2,152,256]{3,2,1,0:T(8,128)(2,1)S(1)}, u32[]{:S(2)}, u32[]{:S(2)}) collective-permute-start(bf16[1,2,152,256]{3,2,1,0:T(8,128)(2,1)S(1)} %copy-done.7), channel_id=1, source_target_pairs={{0,16},{16,0},{32,48},{48,32},{64,80},{80,64},{96,112},{112,96},{1... | collective-permute-start | bytes 466952 | tf_op jit(solution)/shard_map/ppermute | solution.py:16
  67.9 3.0 %copy-start.1 = (f32[2,3072,304]{1,2,0:T(8,128)}, f32[2,3072,304]{1,2,0:T(8,128)S(1)}, u32[]{:S(2)}) copy-start(f32[2,3072,304]{1,2,0:T(8,128)S(1)} %get-tuple-element.18) | copy-start | bytes 22413316
  73.9 24.3 %all-to-all-start.2 = ((f32[32,1,192]{2,1,0:T(1,128)}), f32[32,1,192]{2,1,0:T(1,128)S(1)}, u32[]{:S(2)}, u32[]{:S(2)}) async-start(f32[32,1,192]{2,1,0:T(1,128)} %reshape.118), calls=%async_computation.2 | async-start | bytes 65536 | tf_op jit(solution)/shard_map/all_to_all | solution.py:105
  89.4 18.3 %copy-start.3 = (s32[13,48,48]{2,1,0:T(8,128)S(1)}, s32[13,48,48]{2,1,0:T(8,128)}, u32[]{:S(2)}) copy-start(s32[13,48,48]{2,1,0:T(8,128)} %param.12) | copy-start | bytes 359428
  89.4 18.6 %copy-start.2 = (bf16[13,2,48,256]{3,2,1,0:T(8,128)(2,1)S(1)}, bf16[13,2,48,256]{3,2,1,0:T(8,128)(2,1)}, u32[]{:S(2)}) copy-start(bf16[13,2,48,256]{3,2,1,0:T(8,128)(2,1)} %param.11) | copy-start | bytes 1916932
  94.4 15.3 %copy-start.6 = (s32[13,1]{0,1:T(1,128)S(1)}, s32[13,1]{0,1:T(1,128)}, u32[]{:S(2)}) copy-start(s32[13,1]{0,1:T(1,128)} %param.13) | copy-start | bytes 160
  98.2 9.3 %copy-start.5 = (f32[32,1,192]{2,1,0:T(1,128)}, f32[32,1,192]{2,1,0:T(1,128)S(1)}, u32[]{:S(2)}) copy-start(f32[32,1,192]{2,1,0:T(1,128)S(1)} %all-to-all-done.2) | copy-start | bytes 73732
  98.2 46.1 %all-to-all-start.1 = ((bf16[32,2,48,256]{3,2,1,0:T(8,128)(2,1)}), bf16[32,2,48,256]{3,2,1,0:T(8,128)(2,1)}, u32[]{:S(2)}, u32[]{:S(2)}) async-start(bf16[32,2,48,256]{3,2,1,0:T(8,128)(2,1)} %convert_element_type.40), calls=%async_computation.1 | async-start | bytes 3145728 | tf_op jit(solution)/shard_map/all_to_all | solution.py:98
  107.6 101.9 %all-gather.2.cloned.1.call-start = ((), (), s32[]{:S(2)}) async-start(), calls=%async_computation.3 | async-start | bytes 5431296 | tf_op jit(solution)/shard_map/all_gather | solution.py:124
Sparse Core Ops, SparseCore 0:
  150.2 59.2 all-gather.1
where the time goes:
time: 222 us; the launch traced here: 221 us
  waiting for transfers between devices  113 us (51%)
  starting transfers between devices  34.5 us (16%)
  local copies, waits for them, and re-layouts  28.8 us (13%)
  matrix products  18.6 us (8%)
  between operations  15.6 us (7%)
  other arithmetic  10.1 us (5%)
    all_gather x1, waiting for transfers between devices, local(): lax.all_gather(attn, 'tp', axis=1, tiled=True)  55.3 us
    ppermute x2, waiting for transfers between devices, swapped(): return lax.ppermute(value, axis, pairs)  31.6 us
    all_to_all x1, waiting for transfers between devices, local(): lax.all_to_all(normed.reshape(groups, per_group, TREE, local_cols), 'rep'...  26.3 us
    all_to_all x1, starting transfers between devices, local(): lax.all_to_all(outbound, 'rep', split_axis=0, concat_axis=0, tiled=True)  10.6 us
    all_to_all x1, starting transfers between devices, local(): lax.all_to_all(normed.reshape(groups, per_group, TREE, local_cols), 'rep'...  9.33 us
    all_to_all x1, starting transfers between devices, local(): lax.all_to_all(lse.reshape(groups, per_group, TREE, heads_here), 'rep', s...  9.06 us
    convert_element_type x2, local copies, waits for them, and re-layouts, prompt_attend(): return (normed.reshape(query_rows.shape).astype(jnp.bfloat16), lse)  8.75 us
    dot_general x1, matrix products, prompt_attend(): jnp.einsum('hqk,khd->qhd', raw.astype(jnp.bfloat16), v, preferred_element...  6.44 us
  transfers between devices with their start and end apart: 6, of which 4 were waited for; matrix products, arithmetic and copies ran while one was open for 13% of the time, Pallas kernels for 0%

commit v1 on v0

--- a/solution.py
+++ b/solution.py
@@ -8,6 +8,22 @@
 TREE = 48
 PCAP = 152
 NEG_FILL = -1e30
+
+
+def ring_gather(x, axis, dim):
+    ways, here, step = (lax.axis_size(axis), lax.axis_index(axis), x.shape[dim])
+    dims = [n * ways if d == dim else n for d, n in enumerate(x.shape)]
+    full = lax.dynamic_update_slice_in_dim(jnp.zeros(dims, x.dtype), x, here * step, axis=dim)
+    going_up = going_down = x
+    for far in range(1, ways // 2 + 1):
+        going_up = lax.ppermute(going_up, axis, [(d, (d + 1) % ways) for d in range(ways)])
+        full = lax.dynamic_update_slice_in_dim(full, going_up, (here - far) % ways * step, axis=dim)
+        if 2 * far < ways:
+            going_down = lax.ppermute(going_down, axis, [(d, (d - 1) % ways) for d in range(ways)])
+            full = lax.dynamic_update_slice_in_dim(
+                full, going_down, (here + far) % ways * step, axis=dim
+            )
+    return full
 
 
 def swapped(value, axis, apart):
@@ -120,11 +136,7 @@
     totals = factor_remote + tree_total * factor_tree
     accum = remote_out * factor_remote[..., None] + tree_accum * factor_tree[..., None]
     attn = (accum / totals[..., None]).reshape(req_here * TREE, local_cols).astype(jnp.bfloat16)
-    summed = jnp.dot(
-        lax.all_gather(attn, "tp", axis=1, tiled=True),
-        out_weight,
-        preferred_element_type=jnp.float32,
-    )
+    summed = jnp.dot(ring_gather(attn, "tp", 1), out_weight, preferred_element_type=jnp.float32)
     projected = summed.astype(jnp.bfloat16).reshape(req_here, TREE, out_weight.shape[1])
     accepted_cache = jnp.take_along_axis(tree_cache, accepted_path[:, None, :, None], axis=2)
     return (projected, accepted_cache)

time: 222 us -> 213 us (0.959)
  the two profiles are of different devices: /device:TPU:1 before, /device:TPU:8 now
where the time goes in v1:
time: 213 us; the launch traced here: 212 us
  waiting for transfers between devices  93.7 us (44%)
  starting transfers between devices  57.2 us (27%)
  local copies, waits for them, and re-layouts  32.8 us (15%)
  matrix products  16.2 us (8%)
  other arithmetic  10.1 us (5%)
  between operations  2.42 us (1%)
    ppermute x2, waiting for transfers between devices, swapped(): return lax.ppermute(value, axis, pairs)  30.1 us
    all_to_all x1, waiting for transfers between devices, local(): lax.all_to_all(normed.reshape(groups, per_group, TREE, local_cols), 'rep'...  28.7 us
    ppermute x7, starting transfers between devices, ring_gather(): lax.ppermute(going_down, axis, [(d, (d - 1) % ways) for d in range(ways)])  24.2 us
    ppermute x8, waiting for transfers between devices, ring_gather(): lax.ppermute(going_up, axis, [(d, (d + 1) % ways) for d in range(ways)])  18 us
    ppermute x7, waiting for transfers between devices, ring_gather(): lax.ppermute(going_down, axis, [(d, (d - 1) % ways) for d in range(ways)])  13.8 us
    all_to_all x1, starting transfers between devices, local(): lax.all_to_all(outbound, 'rep', split_axis=0, concat_axis=0, tiled=True)  10.2 us
    all_to_all x1, starting transfers between devices, local(): lax.all_to_all(normed.reshape(groups, per_group, TREE, local_cols), 'rep'...  9.85 us
    convert_element_type x2, local copies, waits for them, and re-layouts, prompt_attend(): return (normed.reshape(query_rows.shape).astype(jnp.bfloat16), lse)  8.74 us
  transfers between devices with their start and end apart: 20, of which 17 were waited for; matrix products, arithmetic and copies ran while one was open for 16% of the time, Pallas kernels for 0%

profile of v1, /device:TPU:8, one launch (start us, length us, event | category | flops | bytes accessed | tf_op | source)
XLA Modules:
  0.0 212.3 jit_solution(3414514757195489593)
XLA Ops:
  0.7 1.0 convert_reduce_fusion
  1.7 0.7 multiply_add_fusion
  2.3 1.7 convolution_convert_fusion
  4.0 2.0 copy.57
  6.0 10.2 %all-to-all-start = ((bf16[32,2,48,256]{3,2,1,0:T(8,128)(2,1)}), bf16[32,2,48,256]{3,2,1,0:T(8,128)(2,1)}, u32[]{:S(2)}, u32[]{:S(2)}) async-start(bf16[32,2,48,256]{3,2,1,0:T(8,128)(2,1)} %bitcast.103), calls=%async_computation | async-start | bytes 3145728 | tf_op jit(solution)/shard_map/all_to_all | solution.py:108
  16.9 2.2 %collective-permute-start.1 = (bf16[152]{0:T(256)(128)(2,1)S(1)}, bf16[152]{0:T(256)(128)(2,1)S(1)}, u32[]{:S(2)}, u32[]{:S(2)}) collective-permute-start(bf16[152]{0:T(256)(128)(2,1)S(1)} %compare_convert_fusion), channel_id=1, source_target_pairs={{0,16},{16,0},{32,48},{48,32},{64,80},{80,64},{96,112},{112,96},{1... | collective-permute-start | bytes 920 | tf_op jit(solution)/shard_map/ppermute | solution.py:32
  19.1 3.6 %collective-permute-start = (bf16[1,2,152,256]{3,2,1,0:T(8,128)(2,1)S(1)}, bf16[1,2,152,256]{3,2,1,0:T(8,128)(2,1)S(1)}, u32[]{:S(2)}, u32[]{:S(2)}) collective-permute-start(bf16[1,2,152,256]{3,2,1,0:T(8,128)(2,1)S(1)} %copy-done.9), channel_id=1, source_target_pairs={{0,16},{16,0},{32,48},{48,32},{64,80},{80,64},{96,112},{112,96},{1... | collective-permute-start | bytes 466952 | tf_op jit(solution)/shard_map/ppermute | solution.py:32
  23.6 26.9 %collective-permute-done.1 = bf16[152]{0:T(256)(128)(2,1)S(1)} collective-permute-done((bf16[152]{0:T(256)(128)(2,1)S(1)}, bf16[152]{0:T(256)(128)(2,1)S(1)}, u32[]{:S(2)}, u32[]{:S(2)}) %collective-permute-start.1) | collective-permute-done | bytes 336 | tf_op jit(solution)/shard_map/ppermute | solution.py:32
  50.5 3.2 %collective-permute-done = bf16[1,2,152,256]{3,2,1,0:T(8,128)(2,1)S(1)} collective-permute-done((bf16[1,2,152,256]{3,2,1,0:T(8,128)(2,1)S(1)}, bf16[1,2,152,256]{3,2,1,0:T(8,128)(2,1)S(1)}, u32[]{:S(2)}, u32[]{:S(2)}) %collective-permute-start) | collective-permute-done | bytes 155680 | tf_op jit(solution)/shard_map/ppermute | solution.py:32
  53.8 3.1 %all-to-all-done = bf16[32,2,48,256]{3,2,1,0:T(8,128)(2,1)} async-done(((bf16[32,2,48,256]{3,2,1,0:T(8,128)(2,1)}), bf16[32,2,48,256]{3,2,1,0:T(8,128)(2,1)}, u32[]{:S(2)}, u32[]{:S(2)}) %all-to-all-start) | async-done | bytes 1572896 | tf_op jit(solution)/shard_map/all_to_all | solution.py:108
  56.9 3.5 %reshape_reshape.3 = bf16[3072,2,128]{2,1,0:T(2,128)(2,1)} reshape(bf16[32,2,48,256]{3,2,1,0:T(8,128)(2,1)} %all-to-all-done) | data formatting | bytes 3145728 | tf_op jit(solution)/shard_map/reshape;reshape | solution.py:36
  60.4 2.6 %fusion = (f32[2,3072]{1,0:T(2,128)S(1)}, f32[2,3072,304]{1,2,0:T(8,128)S(1)}) fusion(pred[304]{0:T(512)(128)(4,1)S(1)} %pad_add_fusion, bf16[152,2,128]{2,0,1:T(8,128)(2,1)S(1)} %copy.42, bf16[152,2,128]{2,0,1:T(8,128)(2,1)S(1)} %copy.41, bf16[3072,2,128]{2,1,0:T(2,128)(2,1)} %reshape_reshape.3), kind=kOutput, calls=%fused_computation.5 | convolution fusion | flops 484059136 | bytes 9224496 | tf_op jit(solution)/shard_map/qhd,khd->hqk/dot_general | solution.py:43
  63.1 3.0 %copy-done.1 = f32[2,3072,304]{1,2,0:T(8,128)} copy-done((f32[2,3072,304]{1,2,0:T(8,128)}, f32[2,3072,304]{1,2,0:T(8,128)S(1)}, u32[]{:S(2)}) %copy-start.1) | copy-done | bytes 7471128
  66.1 2.0 fusion.1
  68.3 0.8 reshape.118
  69.1 7.0 %all-to-all-start.2 = ((f32[32,1,192]{2,1,0:T(1,128)}), f32[32,1,192]{2,1,0:T(1,128)S(1)}, u32[]{:S(2)}, u32[]{:S(2)}) async-start(f32[32,1,192]{2,1,0:T(1,128)} %reshape.118), calls=%async_computation.2 | async-start | bytes 65536 | tf_op jit(solution)/shard_map/all_to_all | solution.py:121
  76.1 6.4 %divide_convert_fusion = bf16[3072,2,128]{0,2,1:T(8,128)(2,1)} fusion(f32[2,3072,304]{1,2,0:T(8,128)} %copy-done.1, f32[2,3072]{1,0:T(2,128)S(1)} %get-tuple-element.17, pred[304]{0:T(512)(128)(4,1)S(1)} %pad_add_fusion, f32[3072,2]{0,1:T(2,128)S(1)} %bitcast.110, bf16[152,2,128]{2,0,1:T(8,128)(2,1)S(1)} %copy.38, bf16[152,2,128]{2,0,1:T(8,128)(2,1)S(1)} %copy.37), kind=kOutput, calls=%fused_computation.14 | convolution fusion | flops 489373696 | bytes 9249072 | tf_op jit(solution)/shard_map/hqk,khd->qhd/dot_general | solution.py:50
  82.6 5.0 %copy.44 = bf16[3072,2,128]{2,1,0:T(2,128)(2,1)} copy(bf16[3072,2,128]{0,2,1:T(8,128)(2,1)} %divide_convert_fusion) | data formatting | bytes 3145728 | tf_op jit(solution)/shard_map/convert_element_type | solution.py:55
  87.5 3.7 %convert_element_type.40 = bf16[32,2,48,256]{3,2,1,0:T(8,128)(2,1)} reshape(bf16[3072,2,128]{2,1,0:T(2,128)(2,1)} %copy.44) | data formatting | bytes 3145728 | tf_op jit(solution)/shard_map/convert_element_type | solution.py:55
  91.3 0.6 copy-done.7
  91.9 9.8 %all-to-all-start.1 = ((bf16[32,2,48,256]{3,2,1,0:T(8,128)(2,1)}), bf16[32,2,48,256]{3,2,1,0:T(8,128)(2,1)}, u32[]{:S(2)}, u32[]{:S(2)}) async-start(bf16[32,2,48,256]{3,2,1,0:T(8,128)(2,1)} %convert_element_type.40), calls=%async_computation.1 | async-start | bytes 3145728 | tf_op jit(solution)/shard_map/all_to_all | solution.py:114
  102.1 0.8 reshape_squeeze.6
  102.9 0.8 reshape_squeeze.7
  103.7 0.5 and_bitcast_fusion
  104.2 0.6 pad_clamp_fusion
  104.8 1.4 fusion.54
  106.2 0.8 fusion.18
  107.0 0.6 broadcast.106
  107.5 2.1 reduce
  109.6 0.9 reshape.119
  110.5 0.7 gather_fusion.1
  111.2 0.8 fusion.38
  112.0 28.7 %all-to-all-done.1 = bf16[32,2,48,256]{3,2,1,0:T(8,128)(2,1)} async-done(((bf16[32,2,48,256]{3,2,1,0:T(8,128)(2,1)}), bf16[32,2,48,256]{3,2,1,0:T(8,128)(2,1)}, u32[]{:S(2)}, u32[]{:S(2)}) %all-to-all-start.1) | async-done | bytes 1572896 | tf_op jit(solution)/shard_map/all_to_all | solution.py:114
  140.7 2.8 %gather_fusion = bf16[13,48,256]{2,1,0:T(8,128)(2,1)} fusion(bf16[64,48,256]{2,1,0:T(8,128)(2,1)} %bitcast.9, s32[1024]{0:T(1024)} %pad_clamp_fusion), kind=kCustom, calls=%fused_computation | custom fusion | bytes 639028 | tf_op jit(solution)/shard_map/jit(_take)/gather | solution.py:128
  143.5 1.8 fusion.17
  145.7 5.9 %collective-permute-start.3 = (bf16[624,256]{1,0:T(8,128)(2,1)S(1)}, bf16[624,256]{1,0:T(8,128)(2,1)}, u32[]{:S(2)}, u32[]{:S(2)}) collective-permute-start(bf16[624,256]{1,0:T(8,128)(2,1)S(1)} %bitcast.108), channel_id=1, source_target_pairs={{0,15},{1,0},{2,1},{3,2},{4,3},{5,4},{6,5},{7,6},{8,7},{9,8},{10,9... | collective-permute-start | bytes 958472 | tf_op jit(solution)/shard_map/ppermute | solution.py:22
  151.6 4.6 %collective-permute-done.2 = bf16[624,256]{1,0:T(8,128)(2,1)S(1)} collective-permute-done((bf16[624,256]{1,0:T(8,128)(2,1)S(1)}, bf16[624,256]{1,0:T(8,128)(2,1)S(1)}, u32[]{:S(2)}, u32[]{:S(2)}) %collective-permute-start.2) | collective-permute-done | bytes 319520 | tf_op jit(solution)/shard_map/ppermute | solution.py:19
  156.3 0.7 bitcast_or_fusion
  157.0 3.0 %collective-permute-start.5 = (bf16[624,256]{1,0:T(8,128)(2,1)}, bf16[624,256]{1,0:T(8,128)(2,1)}, u32[]{:S(2)}, u32[]{:S(2)}) collective-permute-start(bf16[624,256]{1,0:T(8,128)(2,1)} %collective-permute-done.3), channel_id=1, source_target_pairs={{0,15},{1,0},{2,1},{3,2},{4,3},{5,4},{6,5},{7,6},{8,7},{9,8},{10,9... | collective-permute-start | bytes 958472 | tf_op jit(solution)/shard_map/ppermute | solution.py:22
  159.9 4.0 %collective-permute-done.4 = bf16[624,256]{1,0:T(8,128)(2,1)S(1)} collective-permute-done((bf16[624,256]{1,0:T(8,128)(2,1)S(1)}, bf16[624,256]{1,0:T(8,128)(2,1)S(1)}, u32[]{:S(2)}, u32[]{:S(2)}) %collective-permute-start.4) | collective-permute-done | bytes 319520 | tf_op jit(solution)/shard_map/ppermute | solution.py:19
  163.9 0.7 compare_and_fusion
  164.8 1.6 gather_fusion.2
  166.6 0.7 copy.55
  167.3 3.0 %collective-permute-start.7 = (bf16[624,256]{1,0:T(8,128)(2,1)}, bf16[624,256]{1,0:T(8,128)(2,1)S(1)}, u32[]{:S(2)}, u32[]{:S(2)}) collective-permute-start(bf16[624,256]{1,0:T(8,128)(2,1)} %collective-permute-done.5), channel_id=1, source_target_pairs={{0,15},{1,0},{2,1},{3,2},{4,3},{5,4},{6,5},{7,6},{8,7},{9,8},{10,9... | collective-permute-start | bytes 958472 | tf_op jit(solution)/shard_map/ppermute | solution.py:22
  170.2 1.4 collective-permute-done.6
  171.6 0.6 broadcast_in_dim.82
  172.4 2.7 %collective-permute-done.7 = bf16[624,256]{1,0:T(8,128)(2,1)S(1)} collective-permute-done((bf16[624,256]{1,0:T(8,128)(2,1)}, bf16[624,256]{1,0:T(8,128)(2,1)S(1)}, u32[]{:S(2)}, u32[]{:S(2)}) %collective-permute-start.7) | collective-permute-done | bytes 319520 | tf_op jit(solution)/shard_map/ppermute | solution.py:22
  175.0 3.0 %collective-permute-start.9 = (bf16[624,256]{1,0:T(8,128)(2,1)S(1)}, bf16[624,256]{1,0:T(8,128)(2,1)S(1)}, u32[]{:S(2)}, u32[]{:S(2)}) collective-permute-start(bf16[624,256]{1,0:T(8,128)(2,1)S(1)} %collective-permute-done.7), channel_id=1, source_target_pairs={{0,15},{1,0},{2,1},{3,2},{4,3},{5,4},{6,5},{7,6},{8,7},{9,8},{10,9... | collective-permute-start | bytes 958472 | tf_op jit(solution)/shard_map/ppermute | solution.py:22
  178.1 1.0 constant_dynamic-update-slice_fusion.13
  179.1 0.4 collective-permute-done.8
  179.5 1.0 constant_dynamic-update-slice_fusion.11
  180.5 2.0 collective-permute-done.9
  182.6 3.1 %collective-permute-start.11 = (bf16[624,256]{1,0:T(8,128)(2,1)S(1)}, bf16[624,256]{1,0:T(8,128)(2,1)S(1)}, u32[]{:S(2)}, u32[]{:S(2)}) collective-permute-start(bf16[624,256]{1,0:T(8,128)(2,1)S(1)} %collective-permute-done.9), channel_id=1, source_target_pairs={{0,15},{1,0},{2,1},{3,2},{4,3},{5,4},{6,5},{7,6},{8,7},{9,8},{10,9... | collective-permute-start | bytes 958472 | tf_op jit(solution)/shard_map/ppermute | solution.py:22
  185.7 1.0 constant_dynamic-update-slice_fusion.10
  186.7 0.4 collective-permute-done.10
  187.2 3.0 %collective-permute-done.11 = bf16[624,256]{1,0:T(8,128)(2,1)S(1)} collective-permute-done((bf16[624,256]{1,0:T(8,128)(2,1)S(1)}, bf16[624,256]{1,0:T(8,128)(2,1)S(1)}, u32[]{:S(2)}, u32[]{:S(2)}) %collective-permute-start.11) | collective-permute-done | bytes 319520 | tf_op jit(solution)/shard_map/ppermute | solution.py:22
  190.2 3.1 %collective-permute-start.13 = (bf16[624,256]{1,0:T(8,128)(2,1)S(1)}, bf16[624,256]{1,0:T(8,128)(2,1)S(1)}, u32[]{:S(2)}, u32[]{:S(2)}) collective-permute-start(bf16[624,256]{1,0:T(8,128)(2,1)S(1)} %collective-permute-done.11), channel_id=1, source_target_pairs={{0,15},{1,0},{2,1},{3,2},{4,3},{5,4},{6,5},{7,6},{8,7},{9,8},{10,9... | collective-permute-start | bytes 958472 | tf_op jit(solution)/shard_map/ppermute | solution.py:22
  193.3 1.4 collective-permute-done.12
  194.8 3.0 %collective-permute-done.13 = bf16[624,256]{1,0:T(8,128)(2,1)S(1)} collective-permute-done((bf16[624,256]{1,0:T(8,128)(2,1)S(1)}, bf16[624,256]{1,0:T(8,128)(2,1)S(1)}, u32[]{:S(2)}, u32[]{:S(2)}) %collective-permute-start.13) | collective-permute-done | bytes 319520 | tf_op jit(solution)/shard_map/ppermute | solution.py:22
  197.8 3.1 %collective-permute-start.15 = (bf16[624,256]{1,0:T(8,128)(2,1)S(1)}, bf16[624,256]{1,0:T(8,128)(2,1)S(1)}, u32[]{:S(2)}, u32[]{:S(2)}) collective-permute-start(bf16[624,256]{1,0:T(8,128)(2,1)S(1)} %collective-permute-done.13), channel_id=1, source_target_pairs={{0,15},{1,0},{2,1},{3,2},{4,3},{5,4},{6,5},{7,6},{8,7},{9,8},{10,9... | collective-permute-start | bytes 958472 | tf_op jit(solution)/shard_map/ppermute | solution.py:22
  201.0 1.4 collective-permute-done.14
  202.4 3.0 %collective-permute-done.15 = bf16[624,256]{1,0:T(8,128)(2,1)S(1)} collective-permute-done((bf16[624,256]{1,0:T(8,128)(2,1)S(1)}, bf16[624,256]{1,0:T(8,128)(2,1)S(1)}, u32[]{:S(2)}, u32[]{:S(2)}) %collective-permute-start.15) | collective-permute-done | bytes 319520 | tf_op jit(solution)/shard_map/ppermute | solution.py:22
  205.5 4.5 %collective-permute-done.16 = bf16[624,256]{1,0:T(8,128)(2,1)S(1)} collective-permute-done((bf16[624,256]{1,0:T(8,128)(2,1)S(1)}, bf16[624,256]{1,0:T(8,128)(2,1)S(1)}, u32[]{:S(2)}, u32[]{:S(2)}) %collective-permute-start.16) | collective-permute-done | bytes 319520 | tf_op jit(solution)/shard_map/ppermute | solution.py:19
  210.0 2.2 %convolution_convert_fusion.1 = bf16[624,256]{1,0:T(8,128)(2,1)} fusion(bf16[624,4096]{1,0:T(8,128)(2,1)S(1)} %constant_dynamic-update-slice_fusion, bf16[4096,256]{1,0:T(8,128)(2,1)S(1)} %copy-done), kind=kOutput, calls=%fused_computation.25 | convolution fusion | flops 1308782592 | bytes 7528448 | tf_op jit(solution)/shard_map/dot_general | solution.py:139
  (68 shorter events, 2.0 us)
Async XLA Ops:
  0.6 209.4 %copy-start = (bf16[4096,256]{1,0:T(8,128)(2,1)S(1)}, bf16[4096,256]{1,0:T(8,128)(2,1)}, u32[]{:S(2)}) copy-start(bf16[4096,256]{1,0:T(8,128)(2,1)} %param.19) | copy-start | bytes 6291460
  0.6 18.5 %copy-start.9 = (bf16[1,2,152,256]{3,2,1,0:T(8,128)(2,1)S(1)}, bf16[1,2,152,256]{3,2,1,0:T(8,128)(2,1)}, u32[]{:S(2)}) copy-start(bf16[1,2,152,256]{3,2,1,0:T(8,128)(2,1)} %param.17) | copy-start | bytes 466948
  0.7 22.8 %copy-start.6 = (bf16[1,2,152,256]{3,2,1,0:T(8,128)(2,1)S(1)}, bf16[1,2,152,256]{3,2,1,0:T(8,128)(2,1)}, u32[]{:S(2)}) copy-start(bf16[1,2,152,256]{3,2,1,0:T(8,128)(2,1)} %param.15) | copy-start | bytes 466948
  6.0 50.9 %all-to-all-start = ((bf16[32,2,48,256]{3,2,1,0:T(8,128)(2,1)}), bf16[32,2,48,256]{3,2,1,0:T(8,128)(2,1)}, u32[]{:S(2)}, u32[]{:S(2)}) async-start(bf16[32,2,48,256]{3,2,1,0:T(8,128)(2,1)} %bitcast.103), calls=%async_computation | async-start | bytes 3145728 | tf_op jit(solution)/shard_map/all_to_all | solution.py:108
  16.9 33.5 %collective-permute-start.1 = (bf16[152]{0:T(256)(128)(2,1)S(1)}, bf16[152]{0:T(256)(128)(2,1)S(1)}, u32[]{:S(2)}, u32[]{:S(2)}) collective-permute-start(bf16[152]{0:T(256)(128)(2,1)S(1)} %compare_convert_fusion), channel_id=1, source_target_pairs={{0,16},{16,0},{32,48},{48,32},{64,80},{80,64},{96,112},{112,96},{1... | collective-permute-start | bytes 920 | tf_op jit(solution)/shard_map/ppermute | solution.py:32
  19.1 34.6 %collective-permute-start = (bf16[1,2,152,256]{3,2,1,0:T(8,128)(2,1)S(1)}, bf16[1,2,152,256]{3,2,1,0:T(8,128)(2,1)S(1)}, u32[]{:S(2)}, u32[]{:S(2)}) collective-permute-start(bf16[1,2,152,256]{3,2,1,0:T(8,128)(2,1)S(1)} %copy-done.9), channel_id=1, source_target_pairs={{0,16},{16,0},{32,48},{48,32},{64,80},{80,64},{96,112},{112,96},{1... | collective-permute-start | bytes 466952 | tf_op jit(solution)/shard_map/ppermute | solution.py:32
  63.1 3.0 %copy-start.1 = (f32[2,3072,304]{1,2,0:T(8,128)}, f32[2,3072,304]{1,2,0:T(8,128)S(1)}, u32[]{:S(2)}) copy-start(f32[2,3072,304]{1,2,0:T(8,128)S(1)} %get-tuple-element.18) | copy-start | bytes 22413316
  69.1 22.2 %all-to-all-start.2 = ((f32[32,1,192]{2,1,0:T(1,128)}), f32[32,1,192]{2,1,0:T(1,128)S(1)}, u32[]{:S(2)}, u32[]{:S(2)}) async-start(f32[32,1,192]{2,1,0:T(1,128)} %reshape.118), calls=%async_computation.2 | async-start | bytes 65536 | tf_op jit(solution)/shard_map/all_to_all | solution.py:121
  82.5 19.2 %copy-start.3 = (s32[13,48,48]{2,1,0:T(8,128)S(1)}, s32[13,48,48]{2,1,0:T(8,128)}, u32[]{:S(2)}) copy-start(s32[13,48,48]{2,1,0:T(8,128)} %param.12) | copy-start | bytes 359428
  82.5 19.5 %copy-start.2 = (bf16[13,2,48,256]{3,2,1,0:T(8,128)(2,1)S(1)}, bf16[13,2,48,256]{3,2,1,0:T(8,128)(2,1)}, u32[]{:S(2)}) copy-start(bf16[13,2,48,256]{3,2,1,0:T(8,128)(2,1)} %param.11) | copy-start | bytes 1916932
  87.5 16.1 %copy-start.8 = (s32[13,1]{0,1:T(1,128)S(1)}, s32[13,1]{0,1:T(1,128)}, u32[]{:S(2)}) copy-start(s32[13,1]{0,1:T(1,128)} %param.13) | copy-start | bytes 160
  91.3 0.6 copy-start.7
  91.9 48.8 %all-to-all-start.1 = ((bf16[32,2,48,256]{3,2,1,0:T(8,128)(2,1)}), bf16[32,2,48,256]{3,2,1,0:T(8,128)(2,1)}, u32[]{:S(2)}, u32[]{:S(2)}) async-start(bf16[32,2,48,256]{3,2,1,0:T(8,128)(2,1)} %convert_element_type.40), calls=%async_computation.1 | async-start | bytes 3145728 | tf_op jit(solution)/shard_map/all_to_all | solution.py:114
  145.7 10.6 %collective-permute-start.2 = (bf16[624,256]{1,0:T(8,128)(2,1)S(1)}, bf16[624,256]{1,0:T(8,128)(2,1)S(1)}, u32[]{:S(2)}, u32[]{:S(2)}) collective-permute-start(bf16[624,256]{1,0:T(8,128)(2,1)S(1)} %bitcast.107), channel_id=1, source_target_pairs={{0,1},{1,2},{2,3},{3,4},{4,5},{5,6},{6,7},{7,8},{8,9},{9,10},{10,1... | collective-permute-start | bytes 958472 | tf_op jit(solution)/shard_map/ppermute | solution.py:19
  145.7 11.3 %collective-permute-start.3 = (bf16[624,256]{1,0:T(8,128)(2,1)S(1)}, bf16[624,256]{1,0:T(8,128)(2,1)}, u32[]{:S(2)}, u32[]{:S(2)}) collective-permute-start(bf16[624,256]{1,0:T(8,128)(2,1)S(1)} %bitcast.108), channel_id=1, source_target_pairs={{0,15},{1,0},{2,1},{3,2},{4,3},{5,4},{6,5},{7,6},{8,7},{9,8},{10,9... | collective-permute-start | bytes 958472 | tf_op jit(solution)/shard_map/ppermute | solution.py:22
  156.3 7.6 %copy-start.4 = (bf16[624,256]{1,0:T(8,128)(2,1)}, bf16[624,256]{1,0:T(8,128)(2,1)S(1)}, u32[]{:S(2)}) copy-start(bf16[624,256]{1,0:T(8,128)(2,1)S(1)} %collective-permute-done.2) | copy-start | bytes 958468
  156.3 7.6 %collective-permute-start.4 = (bf16[624,256]{1,0:T(8,128)(2,1)S(1)}, bf16[624,256]{1,0:T(8,128)(2,1)S(1)}, u32[]{:S(2)}, u32[]{:S(2)}) collective-permute-start(bf16[624,256]{1,0:T(8,128)(2,1)S(1)} %collective-permute-done.2), channel_id=1, source_target_pairs={{0,1},{1,2},{2,3},{3,4},{4,5},{5,6},{6,7},{7,8},{8,9},{9,10},{10,1... | collective-permute-start | bytes 958472 | tf_op jit(solution)/shard_map/ppermute | solution.py:19
  157.0 10.3 %collective-permute-start.5 = (bf16[624,256]{1,0:T(8,128)(2,1)}, bf16[624,256]{1,0:T(8,128)(2,1)}, u32[]{:S(2)}, u32[]{:S(2)}) collective-permute-start(bf16[624,256]{1,0:T(8,128)(2,1)} %collective-permute-done.3), channel_id=1, source_target_pairs={{0,15},{1,0},{2,1},{3,2},{4,3},{5,4},{6,5},{7,6},{8,7},{9,8},{10,9... | collective-permute-start | bytes 958472 | tf_op jit(solution)/shard_map/ppermute | solution.py:22
  163.9 7.7 %collective-permute-start.6 = (bf16[624,256]{1,0:T(8,128)(2,1)S(1)}, bf16[624,256]{1,0:T(8,128)(2,1)}, u32[]{:S(2)}, u32[]{:S(2)}) collective-permute-start(bf16[624,256]{1,0:T(8,128)(2,1)S(1)} %collective-permute-done.4), channel_id=1, source_target_pairs={{0,1},{1,2},{2,3},{3,4},{4,5},{5,6},{6,7},{7,8},{8,9},{9,10},{10,1... | collective-permute-start | bytes 958472 | tf_op jit(solution)/shard_map/ppermute | solution.py:19
  166.4 5.9 %copy-start.5 = (bf16[624,256]{1,0:T(8,128)(2,1)S(1)}, bf16[624,256]{1,0:T(8,128)(2,1)}, u32[]{:S(2)}) copy-start(bf16[624,256]{1,0:T(8,128)(2,1)} %copy-done.4) | copy-start | bytes 958468
  167.3 7.8 %collective-permute-start.7 = (bf16[624,256]{1,0:T(8,128)(2,1)}, bf16[624,256]{1,0:T(8,128)(2,1)S(1)}, u32[]{:S(2)}, u32[]{:S(2)}) collective-permute-start(bf16[624,256]{1,0:T(8,128)(2,1)} %collective-permute-done.5), channel_id=1, source_target_pairs={{0,15},{1,0},{2,1},{3,2},{4,3},{5,4},{6,5},{7,6},{8,7},{9,8},{10,9... | collective-permute-start | bytes 958472 | tf_op jit(solution)/shard_map/ppermute | solution.py:22
  171.6 7.8 %collective-permute-start.8 = (bf16[624,256]{1,0:T(8,128)(2,1)}, bf16[624,256]{1,0:T(8,128)(2,1)S(1)}, u32[]{:S(2)}, u32[]{:S(2)}) collective-permute-start(bf16[624,256]{1,0:T(8,128)(2,1)} %collective-permute-done.6), channel_id=1, source_target_pairs={{0,1},{1,2},{2,3},{3,4},{4,5},{5,6},{6,7},{7,8},{8,9},{9,10},{10,1... | collective-permute-start | bytes 958472 | tf_op jit(solution)/shard_map/ppermute | solution.py:19
  175.0 7.5 %collective-permute-start.9 = (bf16[624,256]{1,0:T(8,128)(2,1)S(1)}, bf16[624,256]{1,0:T(8,128)(2,1)S(1)}, u32[]{:S(2)}, u32[]{:S(2)}) collective-permute-start(bf16[624,256]{1,0:T(8,128)(2,1)S(1)} %collective-permute-done.7), channel_id=1, source_target_pairs={{0,15},{1,0},{2,1},{3,2},{4,3},{5,4},{6,5},{7,6},{8,7},{9,8},{10,9... | collective-permute-start | bytes 958472 | tf_op jit(solution)/shard_map/ppermute | solution.py:22
  179.5 7.6 %collective-permute-start.10 = (bf16[624,256]{1,0:T(8,128)(2,1)S(1)}, bf16[624,256]{1,0:T(8,128)(2,1)S(1)}, u32[]{:S(2)}, u32[]{:S(2)}) collective-permute-start(bf16[624,256]{1,0:T(8,128)(2,1)S(1)} %collective-permute-done.8), channel_id=1, source_target_pairs={{0,1},{1,2},{2,3},{3,4},{4,5},{5,6},{6,7},{7,8},{8,9},{9,10},{10,1... | collective-permute-start | bytes 958472 | tf_op jit(solution)/shard_map/ppermute | solution.py:19
  182.6 7.6 %collective-permute-start.11 = (bf16[624,256]{1,0:T(8,128)(2,1)S(1)}, bf16[624,256]{1,0:T(8,128)(2,1)S(1)}, u32[]{:S(2)}, u32[]{:S(2)}) collective-permute-start(bf16[624,256]{1,0:T(8,128)(2,1)S(1)} %collective-permute-done.9), channel_id=1, source_target_pairs={{0,15},{1,0},{2,1},{3,2},{4,3},{5,4},{6,5},{7,6},{8,7},{9,8},{10,9... | collective-permute-start | bytes 958472 | tf_op jit(solution)/shard_map/ppermute | solution.py:22
  187.1 7.6 %collective-permute-start.12 = (bf16[624,256]{1,0:T(8,128)(2,1)S(1)}, bf16[624,256]{1,0:T(8,128)(2,1)S(1)}, u32[]{:S(2)}, u32[]{:S(2)}) collective-permute-start(bf16[624,256]{1,0:T(8,128)(2,1)S(1)} %collective-permute-done.10), channel_id=1, source_target_pairs={{0,1},{1,2},{2,3},{3,4},{4,5},{5,6},{6,7},{7,8},{8,9},{9,10},{10,1... | collective-permute-start | bytes 958472 | tf_op jit(solution)/shard_map/ppermute | solution.py:19
  190.2 7.6 %collective-permute-start.13 = (bf16[624,256]{1,0:T(8,128)(2,1)S(1)}, bf16[624,256]{1,0:T(8,128)(2,1)S(1)}, u32[]{:S(2)}, u32[]{:S(2)}) collective-permute-start(bf16[624,256]{1,0:T(8,128)(2,1)S(1)} %collective-permute-done.11), channel_id=1, source_target_pairs={{0,15},{1,0},{2,1},{3,2},{4,3},{5,4},{6,5},{7,6},{8,7},{9,8},{10,9... | collective-permute-start | bytes 958472 | tf_op jit(solution)/shard_map/ppermute | solution.py:22
  194.7 7.6 %collective-permute-start.14 = (bf16[624,256]{1,0:T(8,128)(2,1)S(1)}, bf16[624,256]{1,0:T(8,128)(2,1)S(1)}, u32[]{:S(2)}, u32[]{:S(2)}) collective-permute-start(bf16[624,256]{1,0:T(8,128)(2,1)S(1)} %collective-permute-done.12), channel_id=1, source_target_pairs={{0,1},{1,2},{2,3},{3,4},{4,5},{5,6},{6,7},{7,8},{8,9},{9,10},{10,1... | collective-permute-start | bytes 958472 | tf_op jit(solution)/shard_map/ppermute | solution.py:19
  197.8 7.6 %collective-permute-start.15 = (bf16[624,256]{1,0:T(8,128)(2,1)S(1)}, bf16[624,256]{1,0:T(8,128)(2,1)S(1)}, u32[]{:S(2)}, u32[]{:S(2)}) collective-permute-start(bf16[624,256]{1,0:T(8,128)(2,1)S(1)} %collective-permute-done.13), channel_id=1, source_target_pairs={{0,15},{1,0},{2,1},{3,2},{4,3},{5,4},{6,5},{7,6},{8,7},{9,8},{10,9... | collective-permute-start | bytes 958472 | tf_op jit(solution)/shard_map/ppermute | solution.py:22
  202.3 7.6 %collective-permute-start.16 = (bf16[624,256]{1,0:T(8,128)(2,1)S(1)}, bf16[624,256]{1,0:T(8,128)(2,1)S(1)}, u32[]{:S(2)}, u32[]{:S(2)}) collective-permute-start(bf16[624,256]{1,0:T(8,128)(2,1)S(1)} %collective-permute-done.14), channel_id=1, source_target_pairs={{0,1},{1,2},{2,3},{3,4},{4,5},{5,6},{6,7},{7,8},{8,9},{9,10},{10,1... | collective-permute-start | bytes 958472 | tf_op jit(solution)/shard_map/ppermute | solution.py:19
